TPU v7x, 768 devices: a whole 4x8x12 slice. The times are simulated.
768 devices in a mesh: row: 96 (over z, y_hi, core), col: 8 (over x, y_lo).
Axes of the slice: x: 4, y: 8 (y_hi: 4, y_lo: 2; y = y_hi * 2 + y_lo), z: 12, core: 2. Of those that a mesh axis runs over, the one named last changes fastest.
Arguments:
- features: bfloat16 [98304, 128], P(('row', 'col')), may hold values from -6 to 6
- tiles: bfloat16 [96, 8, 128, 128, 128], P('row', 'col'), may hold values from -0.0625 to 0.0625
- tile_index: int32 [96, 8, 128], P('row', 'col'), may hold values from 0 to 767, as said below
- tile_count: int32 [96, 8], P('row', 'col'), may hold values from 16 to 128, as said below
- w_first: bfloat16 [128, 256], replicated, may hold values from -0.5 to 0.5
- b_first: float32 [256], replicated, may hold values from -3 to 3
- w_second: bfloat16 [256, 128], replicated, may hold values from -0.375 to 0.375
- b_second: float32 [128], replicated, may hold values from -3 to 3
Outputs:
- logits: float32 [98304, 128], P(('row', 'col'))
Inputs may be any that keep to these rules, and one draw needn't show every extreme that they name: `tile_index`: within one device the live slots name distinct tiles. `tile_count`: some device has all 128 slots live; every count is 128 divided by 1, 2, 4 or 8.
All inputs are finite; a program needn't handle non-finite values.
Results may differ from a plain program's by a relative error of at most 0.01.
Values may be sent and summed in bfloat16 or wider, within the bound.
No kernel may reach another device: no remote copies, remote signals or barrier semaphores. Data moves between devices by JAX's collectives and lax.ppermute only.
A program may use at most 32 MiB of HBM per device.

v0:
```python
import jax
import jax.numpy as jnp
from jax import lax
from jax.sharding import PartitionSpec as P


def tile_sum(columns, tile_block, slot_index, live_count, node_rows):
    tile_size = tile_block.shape[-1]
    feat_width = columns.shape[1]
    col_tiles = columns.reshape(columns.shape[0] // tile_size, tile_size, feat_width)
    tile_cols = col_tiles.shape[0]
    row_tiles = lax.axis_size("col") * node_rows // tile_size
    picked = jnp.take(col_tiles, slot_index % tile_cols, axis=0)
    products = jnp.einsum("mab,mbf->maf", tile_block, picked, preferred_element_type=jnp.float32)
    live_mask = jnp.arange(slot_index.shape[0], dtype=jnp.int32) < live_count
    placing = (
        ((slot_index // tile_cols)[:, None] == jnp.arange(row_tiles, dtype=jnp.int32)[None, :])
        & live_mask[:, None]
    ).astype(jnp.float32)
    partial_value = jnp.einsum("mr,maf->raf", placing, products)
    return partial_value.reshape(row_tiles * tile_size, feat_width)


def aggregate(node_feats, tile_block, slot_index, live_count):
    node_rows = node_feats.shape[0]
    gathered = lax.all_gather(node_feats, "row", axis=0, tiled=True)
    partial_value = tile_sum(gathered, tile_block, slot_index, live_count, node_rows)
    totals = lax.psum(partial_value, "col")
    return lax.dynamic_slice_in_dim(totals, lax.axis_index("col") * node_rows, node_rows, 0)


def local(features, tiles, tile_index, tile_count, w_first, b_first, w_second, b_second):
    tile_block = tiles[0, 0]
    slot_index = tile_index[0, 0]
    live_count = tile_count[0, 0]
    first_agg = aggregate(features, tile_block, slot_index, live_count).astype(jnp.bfloat16)
    hidden = jnp.maximum(
        jnp.dot(first_agg, w_first, preferred_element_type=jnp.float32) + b_first, 0.0
    ).astype(jnp.bfloat16)
    projected = jnp.dot(hidden, w_second, preferred_element_type=jnp.float32).astype(jnp.bfloat16)
    second = aggregate(projected, tile_block, slot_index, live_count)
    return second + b_second


def solution(mesh):
    in_specs = (
        P(("row", "col"), None),
        P("row", "col", None, None, None),
        P("row", "col", None),
        P("row", "col"),
        P(),
        P(),
        P(),
        P(),
    )
    out_specs = P(("row", "col"), None)
    return jax.shard_map(local, mesh=mesh, in_specs=in_specs, out_specs=out_specs, check_vma=False)
```

profile of v0, /device:TPU:16, one launch (start us, length us, event | category | flops | bytes accessed | tf_op | source)
XLA Modules:
  0.0 435.9 jit_solution(12398579080114157075)
XLA Ops:
  6.5 0.0 copy-start
  6.5 0.0 all-gather.3.cloned.1.call-start
  6.5 0.7 all-gather.3.cloned.1.call-update
  7.3 0.0 all-gather.5.cloned.1.call-start
  8.0 0.7 compare_and_fusion
  8.7 0.7 fusion.26
  9.3 127.2 %all-gather.3.cloned.1.call-done = bf16[12288,128]{1,0:T(8,128)(2,1)} async-done(((bf16[128,128]{1,0:T(8,128)(2,1)}), bf16[12288,128]{1,0:T(8,128)(2,1)}) %all-gather.3.cloned.1.call-update) | async-done | bytes 3145744 | tf_op jit(solution)/shard_map/all_gather | solution.py:26
  136.6 4.9 %gather_fusion = bf16[128,128,128]{2,1,0:T(8,128)(2,1)} fusion(bf16[96,128,128]{2,1,0:T(8,128)(2,1)} %bitcast.33, s32[1024]{0:T(1024)S(1)} %pad_clamp_fusion), kind=kCustom, calls=%fused_computation.clone | custom fusion | bytes 8389120 | tf_op jit(solution)/shard_map/jit(_take)/gather | solution.py:13
  141.5 8.6 %fusion.6 = bf16[128,128,128]{2,1,0:T(8,128)(2,1)} fusion(bf16[1,1,128,128,128]{4,3,2,1,0:T(8,128)(2,1)} %param.11, bf16[128,128,128]{2,1,0:T(8,128)(2,1)} %gather_fusion, pred[128]{0:T(512)(128)(4,1)S(1)} %get-tuple-element.6), kind=kOutput, calls=%fused_computation.8 | convolution fusion | flops 538968064 | bytes 12583040 | tf_op jit(solution)/shard_map/mab,mbf->maf/dot_general | solution.py:14
  150.1 6.7 %copy.11 = bf16[128,128,128]{1,0,2:T(8,128)(2,1)} copy(bf16[128,128,128]{2,1,0:T(8,128)(2,1)} %fusion.6) | data formatting | bytes 8388608 | tf_op jit(solution)/shard_map/mab,mbf->maf/dot_general | solution.py:14
  156.8 0.0 copy-start.1
  156.8 0.0 copy-start.2
  156.8 2.9 fusion.2
  159.7 0.1 copy.9
  159.8 42.5 %all-reduce.4 = bf16[1024,128]{1,0:T(8,128)(2,1)S(1)} all-reduce(f32[1024,128]{1,0:T(8,128)S(1)} %bitcast.36), channel_id=1, replica_groups=mesh['row'=96,'col'=8] {'col'}, use_global_device_ids=true, to_apply=%region_0.2 | all-reduce | flops 131072 | bytes 786432 | tf_op jit(solution)/shard_map/psum | solution.py:28
  202.3 0.0 copy-done
  202.3 0.0 copy-done.1
  202.3 0.0 copy-done.2
  202.3 0.9 fusion.17
  203.2 0.0 all-gather.5.cloned.1.call-update
  203.2 0.0 all-reduce.3.cloned.1.call-start
  203.3 113.3 %all-gather.5.cloned.1.call-done = bf16[12288,128]{1,0:T(8,128)(2,1)} async-done(((bf16[128,128]{1,0:T(8,128)(2,1)}), bf16[12288,128]{1,0:T(8,128)(2,1)}) %all-gather.5.cloned.1.call-update) | async-done | bytes 3145744 | tf_op jit(solution)/shard_map/all_gather | solution.py:26
  316.6 4.9 %gather_fusion.1 = bf16[128,128,128]{2,1,0:T(8,128)(2,1)} fusion(bf16[96,128,128]{2,1,0:T(8,128)(2,1)} %bitcast.34, s32[1024]{0:T(1024)S(1)} %pad_clamp_fusion), kind=kCustom, calls=%fused_computation.1.clone | custom fusion | bytes 8389120 | tf_op jit(solution)/shard_map/jit(_take)/gather | solution.py:13
  321.5 8.6 %fusion.4 = bf16[128,128,128]{2,1,0:T(8,128)(2,1)} fusion(bf16[1,1,128,128,128]{4,3,2,1,0:T(8,128)(2,1)} %param.11, bf16[128,128,128]{2,1,0:T(8,128)(2,1)} %gather_fusion.1, pred[128]{0:T(512)(128)(4,1)S(1)} %get-tuple-element.6), kind=kOutput, calls=%fused_computation.6 | convolution fusion | flops 538968064 | bytes 12583040 | tf_op jit(solution)/shard_map/mab,mbf->maf/dot_general | solution.py:14
  330.2 6.7 %copy.12 = bf16[128,128,128]{1,0,2:T(8,128)(2,1)} copy(bf16[128,128,128]{2,1,0:T(8,128)(2,1)} %fusion.4) | data formatting | bytes 8388608 | tf_op jit(solution)/shard_map/mab,mbf->maf/dot_general | solution.py:14
  336.9 0.0 copy-start.3
  336.9 2.9 fusion
  339.7 0.9 copy.10
  340.6 0.0 all-reduce.3.cloned.1.call-update
  340.7 87.2 %all-reduce.3.cloned.1.call-done = f32[1024,128]{1,0:T(8,128)} async-done(((f32[1024,128]{1,0:T(8,128)}), f32[1024,128]{1,0:T(8,128)}) %all-reduce.3.cloned.1.call-update) | async-done | bytes 524304 | tf_op jit(solution)/shard_map/psum | solution.py:28
  427.9 0.0 copy-done.3
  427.9 1.5 dynamic-slice_add_fusion
  (2 shorter events, 0.0 us)
Async XLA Ops:
  6.5 195.7 %copy-start = (bf16[256,128]{1,0:T(8,128)(2,1)S(1)}, bf16[256,128]{1,0:T(8,128)(2,1)}, u32[]{:S(2)}) copy-start(bf16[256,128]{1,0:T(8,128)(2,1)} %param.16) | copy-start | bytes 196612
  6.5 130.0 %all-gather.3.cloned.1.call-start = ((), (), s32[]{:S(2)}) async-start(), calls=%async_computation | async-start | bytes 3178496 | tf_op jit(solution)/shard_map/all_gather | solution.py:26
  7.3 309.4 %all-gather.5.cloned.1.call-start = ((), (), s32[]{:S(2)}) async-start(), calls=%async_computation.1 | async-start | bytes 3178496 | tf_op jit(solution)/shard_map/all_gather | solution.py:26
  156.8 45.5 %copy-start.1 = (bf16[128,256]{1,0:T(8,128)(2,1)S(1)}, bf16[128,256]{1,0:T(8,128)(2,1)}, u32[]{:S(2)}) copy-start(bf16[128,256]{1,0:T(8,128)(2,1)} %param.14) | copy-start | bytes 196612
  156.8 45.5 %copy-start.2 = (f32[256]{0:T(256)S(1)}, f32[256]{0:T(256)}, u32[]{:S(2)}) copy-start(f32[256]{0:T(256)} %param.15) | copy-start | bytes 3076
  203.2 224.6 %all-reduce.3.cloned.1.call-start = ((), (), s32[]{:S(2)}) async-start(), calls=%async_computation.2 | async-start | bytes 1048576 | tf_op jit(solution)/shard_map/psum | solution.py:28
  336.9 91.0 %copy-start.3 = (f32[128]{0:T(128)S(1)}, f32[128]{0:T(128)}, u32[]{:S(2)}) copy-start(f32[128]{0:T(128)} %param.17) | copy-start | bytes 1540
Sparse Core Ops, SparseCore 0:
  11.0 125.5 all-gather.2
  203.4 113.2 all-gather.4
  340.8 87.0 all-reduce.2
where the time goes:
time: 436 us
  waiting for transfers between devices  329 us (75%)
  blocking collectives  42.5 us (10%)
  local copies, waits for them, and re-layouts  24.3 us (6%)
  matrix products  23.9 us (5%)
  between operations  13.8 us (3%)
    all_gather x2, waiting for transfers between devices, aggregate(): gathered = lax.all_gather(node_feats, 'row', axis=0, tiled=True)  241 us
    psum x1, waiting for transfers between devices, aggregate(): totals = lax.psum(partial_value, 'col')  87.2 us
    psum x1, blocking collectives, aggregate(): totals = lax.psum(partial_value, 'col')  42.5 us
    dot_general x2, matrix products, tile_sum(): jnp.einsum('mab,mbf->maf', tile_block, picked, preferred_element_type=jnp...  17.3 us
    dot_general x2, local copies, waits for them, and re-layouts, tile_sum(): jnp.einsum('mab,mbf->maf', tile_block, picked, preferred_element_type=jnp...  13.4 us
    gather x2, local copies, waits for them, and re-layouts, tile_sum(): picked = jnp.take(col_tiles, slot_index % tile_cols, axis=0)  9.81 us
  transfers between devices with their start and end apart: 3, of which 3 were waited for; matrix products, arithmetic and copies ran while one was open for 0% of the time, Pallas kernels for 0%

commit v1 on v0

v1 whole, which is shorter than its diff:
```python
import jax
import jax.numpy as jnp
from jax import lax
from jax.experimental import pallas as pl
from jax.experimental.pallas import tpu as pltpu
from jax.sharding import Mesh, PartitionSpec as P

TILE = 128
ROW_TILES = 8
SLOTS = 128
CHUNK = 16
UNROLL = 8
AXES = ("z", "yh", "core", "x", "yl")
SIZES = (12, 4, 2, 4, 2)
ROW = ("z", "yh", "core")
COL = ("x", "yl")


def spmm_kernel(count, rows, cols, tiles, *rest):
    pieces = rest[:4]
    out, tile_buf, feat, acc, sems = rest[4:]
    live = count[0]
    chunks = SLOTS // CHUNK

    def fetch(c):
        part = pl.ds(c * CHUNK, CHUNK)
        return pltpu.make_async_copy(tiles.at[part], tile_buf.at[part], sems.at[c])

    for c in range(chunks):
        @pl.when(c * CHUNK < live)
        def _():
            fetch(c).start()

    depth = pieces[0].shape[0]
    for p, piece in enumerate(pieces):
        feat[p * depth:(p + 1) * depth] = piece[...]
    acc[...] = jnp.zeros_like(acc)
    for c in range(chunks):
        @pl.when(c * CHUNK < live)
        def _():
            fetch(c).wait()

            @pl.loop(0, CHUNK // UNROLL)
            def _(k):
                base = c * CHUNK + k * UNROLL
                products = [
                    jnp.dot(
                        tile_buf[base + u],
                        feat[cols[base + u]],
                        preferred_element_type=jnp.float32,
                    )
                    for u in range(UNROLL)
                ]
                for u in range(UNROLL):
                    acc[rows[base + u]] += products[u]

    out[...] = acc[...].astype(out.dtype)


def spmm(count, rows, cols, tiles, pieces):
    smem = pl.BlockSpec(memory_space=pltpu.SMEM)
    vmem = pl.BlockSpec(memory_space=pltpu.VMEM)
    return pl.pallas_call(
        spmm_kernel,
        out_shape=jax.ShapeDtypeStruct((ROW_TILES, TILE, TILE), jnp.bfloat16),
        in_specs=[smem, smem, smem, pl.BlockSpec(memory_space=pl.ANY)] + [vmem] * 4,
        out_specs=vmem,
        scratch_shapes=[
            pltpu.VMEM((SLOTS, TILE, TILE), jnp.bfloat16),
            pltpu.VMEM((96, TILE, TILE), jnp.bfloat16),
            pltpu.VMEM((ROW_TILES, TILE, TILE), jnp.float32),
            pltpu.SemaphoreType.DMA((SLOTS // CHUNK,)),
        ],
        name="spmm",
    )(count, rows, cols, tiles, *pieces)


def dense_kernel(parts, w_first, b_first, w_second, out):
    total = jnp.sum(parts[...].astype(jnp.float32), axis=0).astype(jnp.bfloat16)
    hidden = jnp.dot(total, w_first[...], preferred_element_type=jnp.float32)
    hidden = jnp.maximum(hidden + b_first[...], 0.0).astype(jnp.bfloat16)
    projected = jnp.dot(hidden, w_second[...], preferred_element_type=jnp.float32)
    out[...] = jnp.broadcast_to(projected.astype(out.dtype)[None], out.shape)


def dense(parts, w_first, b_first, w_second):
    return pl.pallas_call(
        dense_kernel,
        out_shape=jax.ShapeDtypeStruct((4, TILE, TILE), jnp.bfloat16),
        in_specs=[pl.BlockSpec(memory_space=pltpu.VMEM)] * 4,
        out_specs=pl.BlockSpec(memory_space=pltpu.VMEM),
        name="dense",
    )(parts, w_first, b_first[None], w_second)


def gather(copies):
    column = lax.all_to_all(copies, "yh", 0, 0)
    swap = [(0, 1), (1, 0)]
    own = []
    other = []
    for h in range(2):
        half = lax.all_gather(column[2 * h:2 * h + 2], "z", axis=0, tiled=True)
        own.append(half)
        other.append(lax.ppermute(half, "core", swap))
    return own + other


def position(cols):
    core = lax.axis_index("core")
    z = cols // 8
    yh = (cols // 2) % 4
    piece = jnp.where(cols % 2 == core, 0, 2) + yh // 2
    return piece * 24 + z * 2 + yh % 2


def local(features, tiles, tile_index, tile_count, w_first, b_first, w_second, b_second):
    blocks = tiles[0, 0]
    index = tile_index[0, 0]
    count = tile_count[0]
    rows = index // 96
    cols = position(index % 96)

    def aggregate(copies):
        partial = spmm(count, rows, cols, blocks, gather(copies))
        return lax.all_to_all(partial, COL, 0, 0)

    first = aggregate(jnp.broadcast_to(features[None], (4, TILE, TILE)))
    second = aggregate(dense(first, w_first, b_first, w_second))
    return jnp.sum(second.astype(jnp.float32), axis=0) + b_second


def solution(mesh):
    fine = Mesh(mesh.devices.reshape(SIZES), AXES)
    in_specs = (
        P(ROW + COL, None),
        P(ROW, COL, None, None, None),
        P(ROW, COL, None),
        P(ROW, COL),
        P(),
        P(),
        P(),
        P(),
    )
    return jax.shard_map(
        local, mesh=fine, in_specs=in_specs, out_specs=P(ROW + COL, None), check_vma=False
    )
```

time: 436 us -> 196 us (0.45)
  the two profiles are of different devices: /device:TPU:16 before, /device:TPU:64 now
where the time goes in v1:
time: 196 us; the launch traced here: 195 us
  blocking collectives  163 us (83%)
  Pallas kernels  16.9 us (9%)
  starting transfers between devices  8.63 us (4%)
  local copies, waits for them, and re-layouts  2.8 us (1%)
    all_gather x4, blocking collectives, gather(): half = lax.all_gather(column[2 * h:2 * h + 2], 'z', axis=0, tiled=True)  112 us
    all_to_all x2, blocking collectives, gather(): column = lax.all_to_all(copies, 'yh', 0, 0)  27.5 us
    all_to_all x2, blocking collectives, aggregate(): return lax.all_to_all(partial, COL, 0, 0)  23.5 us
    pallas_call x2, Pallas kernels, spmm(): pl.pallas_call(spmm_kernel, out_shape=jax.ShapeDtypeStruct((ROW_TILES, TI...  14.9 us
    ppermute x4, starting transfers between devices, gather(): other.append(lax.ppermute(half, 'core', swap))  8.63 us
  transfers between devices with their start and end apart: 4, of which 1 were waited for; matrix products, arithmetic and copies ran while one was open for 1% of the time, Pallas kernels for 0%

profile of v1, /device:TPU:64, one launch (start us, length us, event | category | flops | bytes accessed | tf_op | source)
XLA Modules:
  0.0 195.5 jit_solution(16243100602414603524)
XLA Ops:
  0.0 0.8 broadcast_in_dim.8
  0.8 15.8 %all_to_all.20 = bf16[4,128,128]{2,1,0:T(8,128)(2,1)S(1)} all-to-all(bf16[4,128,128]{2,1,0:T(8,128)(2,1)S(1)} %broadcast_in_dim.8), channel_id=1, replica_groups=mesh['z'=12,'yh'=4,'core'=2,'x'=4,'yl'=2] {'yh'}, dimensions={0} | all-to-all | bytes 262144 | tf_op jit(solution)/shard_map/all_to_all | solution.py:97
  16.6 34.2 %all_gather.13.rest_1_ = bf16[24,128,128]{2,1,0:T(8,128)(2,1)S(1)} all-gather(bf16[2,128,128]{2,1,0:T(8,128)(2,1)S(1)} %get-tuple-element.7), channel_id=1, replica_groups=mesh['z'=12,'yh'=4,'core'=2,'x'=4,'yl'=2] {'z'}, dimensions={0}, use_global_device_ids=true | all-gather | bytes 851968 | tf_op jit(solution)/shard_map/all_gather | solution.py:102
  50.8 0.0 copy-start
  50.8 26.7 %all_gather.12.rest_0_ = bf16[24,128,128]{2,1,0:T(8,128)(2,1)S(1)} all-gather(bf16[2,128,128]{2,1,0:T(8,128)(2,1)S(1)} %get-tuple-element.8), channel_id=1, replica_groups=mesh['z'=12,'yh'=4,'core'=2,'x'=4,'yl'=2] {'z'}, dimensions={0}, use_global_device_ids=true | all-gather | bytes 851968 | tf_op jit(solution)/shard_map/all_gather | solution.py:102
  77.5 0.0 copy-start.1
  77.5 1.9 collective-permute-start
  79.4 2.4 %collective-permute-start.1 = (bf16[24,128,128]{2,1,0:T(8,128)(2,1)S(1)}, bf16[24,128,128]{2,1,0:T(8,128)(2,1)S(1)}, u32[]{:S(2)}, u32[]{:S(2)}) collective-permute-start(bf16[24,128,128]{2,1,0:T(8,128)(2,1)S(1)} %all_gather.13.rest_1_), channel_id=1, source_target_pairs={{0,8},{8,0},{1,9},{9,1},{2,10},{10,2},{3,11},{11,3},{4,12},{12,4},... | collective-permute-start | bytes 2359304 | tf_op jit(solution)/shard_map/ppermute | solution.py:104
  82.5 1.3 fusion.1
  83.8 0.0 collective-permute-done.rest_2_
  83.8 0.0 copy-start.4
  83.8 0.0 collective-permute-done.1.rest_3_
  83.8 0.0 copy-start.5
  83.8 0.0 copy-done
  83.8 0.0 copy-done.1
  83.8 0.8 copy-done.4
  84.7 0.3 copy-done.5
  84.9 7.5 %spmm.2 = bf16[8,128,128]{2,1,0:T(8,128)(2,1)} custom-call(s32[1]{0:T(128)} %bitcast.14.count, s32[128]{0:T(128)} %get-tuple-element.10.rows, s32[128]{0:T(128)} %get-tuple-element.9.cols, bf16[128,128,128]{2,1,0:T(8,128)(2,1)} %bitcast.16, bf16[24,128,128]{2,1,0:T(8,128)(2,1)} %copy-done.1, bf16[24,128,128]{2,1,0:T(8,128)(2,1)} %copy-done, ...), custom_call_target="tpu_custom_call" | custom-call | tf_op jit(solution)/shard_map/spmm/pallas_call | solution.py:63
  92.4 12.1 %all_to_all.21.parts = bf16[8,128,128]{2,1,0:T(8,128)(2,1)} all-to-all(bf16[8,128,128]{2,1,0:T(8,128)(2,1)} %spmm.2), channel_id=1, replica_groups=mesh['z'=12,'yh'=4,'core'=2,'x'=4,'yl'=2] {'x','yl'}, dimensions={0} | all-to-all | bytes 524288 | tf_op jit(solution)/shard_map/all_to_all | solution.py:125
  104.5 1.9 dense.1
  106.4 11.7 %all_to_all.22 = bf16[4,128,128]{2,1,0:T(8,128)(2,1)S(1)} all-to-all(bf16[4,128,128]{2,1,0:T(8,128)(2,1)} %dense.1), channel_id=1, replica_groups=mesh['z'=12,'yh'=4,'core'=2,'x'=4,'yl'=2] {'yh'}, dimensions={0} | all-to-all | bytes 262144 | tf_op jit(solution)/shard_map/all_to_all | solution.py:97
  118.1 24.0 %all_gather.15.rest_1_ = bf16[24,128,128]{2,1,0:T(8,128)(2,1)S(1)} all-gather(bf16[2,128,128]{2,1,0:T(8,128)(2,1)S(1)} %get-tuple-element.5), channel_id=1, replica_groups=mesh['z'=12,'yh'=4,'core'=2,'x'=4,'yl'=2] {'z'}, dimensions={0}, use_global_device_ids=true | all-gather | bytes 851968 | tf_op jit(solution)/shard_map/all_gather | solution.py:102
  142.1 0.0 copy-start.2
  142.1 26.7 %all_gather.14.rest_0_ = bf16[24,128,128]{2,1,0:T(8,128)(2,1)S(1)} all-gather(bf16[2,128,128]{2,1,0:T(8,128)(2,1)S(1)} %get-tuple-element.6), channel_id=1, replica_groups=mesh['z'=12,'yh'=4,'core'=2,'x'=4,'yl'=2] {'z'}, dimensions={0}, use_global_device_ids=true | all-gather | bytes 851968 | tf_op jit(solution)/shard_map/all_gather | solution.py:102
  168.8 0.0 copy-start.3
  168.8 1.9 collective-permute-start.2
  170.7 2.4 %collective-permute-start.3 = (bf16[24,128,128]{2,1,0:T(8,128)(2,1)S(1)}, bf16[24,128,128]{2,1,0:T(8,128)(2,1)S(1)}, u32[]{:S(2)}, u32[]{:S(2)}) collective-permute-start(bf16[24,128,128]{2,1,0:T(8,128)(2,1)S(1)} %all_gather.15.rest_1_), channel_id=1, source_target_pairs={{0,8},{8,0},{1,9},{9,1},{2,10},{10,2},{3,11},{11,3},{4,12},{12,4},... | collective-permute-start | bytes 2359304 | tf_op jit(solution)/shard_map/ppermute | solution.py:104
  173.1 0.0 collective-permute-done.2.rest_2_
  173.1 0.0 copy-start.6
  173.2 1.9 collective-permute-done.3.rest_3_
  175.0 0.0 copy-start.7
  175.0 0.0 copy-done.2
  175.0 0.0 copy-done.3
  175.0 0.0 copy-done.6
  175.0 0.9 copy-done.7
  175.9 0.0 copy-start.8
  175.9 7.5 %spmm.3 = bf16[8,128,128]{2,1,0:T(8,128)(2,1)} custom-call(s32[1]{0:T(128)} %bitcast.15.count, s32[128]{0:T(128)} %get-tuple-element.10.rows, s32[128]{0:T(128)} %get-tuple-element.9.cols, bf16[128,128,128]{2,1,0:T(8,128)(2,1)} %bitcast.17, bf16[24,128,128]{2,1,0:T(8,128)(2,1)} %copy-done.3, bf16[24,128,128]{2,1,0:T(8,128)(2,1)} %copy-done.2, ...), custom_call_target="tpu_custom_call" | custom-call | tf_op jit(solution)/shard_map/spmm/pallas_call | solution.py:63
  183.4 11.4 %all_to_all.23 = bf16[8,128,128]{2,1,0:T(8,128)(2,1)S(1)} all-to-all(bf16[8,128,128]{2,1,0:T(8,128)(2,1)} %spmm.3), channel_id=1, replica_groups=mesh['z'=12,'yh'=4,'core'=2,'x'=4,'yl'=2] {'x','yl'}, dimensions={0} | all-to-all | bytes 524288 | tf_op jit(solution)/shard_map/all_to_all | solution.py:125
  194.9 0.0 copy-done.8
  194.9 0.6 broadcast_add_fusion
  (3 shorter events, 0.1 us)
Async XLA Ops:
  50.8 33.0 %copy-start = (bf16[24,128,128]{2,1,0:T(8,128)(2,1)}, bf16[24,128,128]{2,1,0:T(8,128)(2,1)S(1)}, u32[]{:S(2)}) copy-start(bf16[24,128,128]{2,1,0:T(8,128)(2,1)S(1)} %all_gather.13.rest_1_) | copy-start | bytes 2359300
  77.5 6.3 %copy-start.1 = (bf16[24,128,128]{2,1,0:T(8,128)(2,1)}, bf16[24,128,128]{2,1,0:T(8,128)(2,1)S(1)}, u32[]{:S(2)}) copy-start(bf16[24,128,128]{2,1,0:T(8,128)(2,1)S(1)} %all_gather.12.rest_0_) | copy-start | bytes 2359300
  77.5 6.2 %collective-permute-start = (bf16[24,128,128]{2,1,0:T(8,128)(2,1)S(1)}, bf16[24,128,128]{2,1,0:T(8,128)(2,1)S(1)}, u32[]{:S(2)}, u32[]{:S(2)}) collective-permute-start(bf16[24,128,128]{2,1,0:T(8,128)(2,1)S(1)} %all_gather.12.rest_0_), channel_id=1, source_target_pairs={{0,8},{8,0},{1,9},{9,1},{2,10},{10,2},{3,11},{11,3},{4,12},{12,4},... | collective-permute-start | bytes 2359304 | tf_op jit(solution)/shard_map/ppermute | solution.py:104
  79.4 4.3 %collective-permute-start.1 = (bf16[24,128,128]{2,1,0:T(8,128)(2,1)S(1)}, bf16[24,128,128]{2,1,0:T(8,128)(2,1)S(1)}, u32[]{:S(2)}, u32[]{:S(2)}) collective-permute-start(bf16[24,128,128]{2,1,0:T(8,128)(2,1)S(1)} %all_gather.13.rest_1_), channel_id=1, source_target_pairs={{0,8},{8,0},{1,9},{9,1},{2,10},{10,2},{3,11},{11,3},{4,12},{12,4},... | collective-permute-start | bytes 2359304 | tf_op jit(solution)/shard_map/ppermute | solution.py:104
  83.8 0.9 copy-start.4
  83.8 1.1 copy-start.5
  142.1 32.9 %copy-start.2 = (bf16[24,128,128]{2,1,0:T(8,128)(2,1)}, bf16[24,128,128]{2,1,0:T(8,128)(2,1)S(1)}, u32[]{:S(2)}) copy-start(bf16[24,128,128]{2,1,0:T(8,128)(2,1)S(1)} %all_gather.15.rest_1_) | copy-start | bytes 2359300
  168.8 6.2 %copy-start.3 = (bf16[24,128,128]{2,1,0:T(8,128)(2,1)}, bf16[24,128,128]{2,1,0:T(8,128)(2,1)S(1)}, u32[]{:S(2)}) copy-start(bf16[24,128,128]{2,1,0:T(8,128)(2,1)S(1)} %all_gather.14.rest_0_) | copy-start | bytes 2359300
  168.8 4.3 %collective-permute-start.2 = (bf16[24,128,128]{2,1,0:T(8,128)(2,1)S(1)}, bf16[24,128,128]{2,1,0:T(8,128)(2,1)S(1)}, u32[]{:S(2)}, u32[]{:S(2)}) collective-permute-start(bf16[24,128,128]{2,1,0:T(8,128)(2,1)S(1)} %all_gather.14.rest_0_), channel_id=1, source_target_pairs={{0,8},{8,0},{1,9},{9,1},{2,10},{10,2},{3,11},{11,3},{4,12},{12,4},... | collective-permute-start | bytes 2359304 | tf_op jit(solution)/shard_map/ppermute | solution.py:104
  170.7 4.3 %collective-permute-start.3 = (bf16[24,128,128]{2,1,0:T(8,128)(2,1)S(1)}, bf16[24,128,128]{2,1,0:T(8,128)(2,1)S(1)}, u32[]{:S(2)}, u32[]{:S(2)}) collective-permute-start(bf16[24,128,128]{2,1,0:T(8,128)(2,1)S(1)} %all_gather.15.rest_1_), channel_id=1, source_target_pairs={{0,8},{8,0},{1,9},{9,1},{2,10},{10,2},{3,11},{11,3},{4,12},{12,4},... | collective-permute-start | bytes 2359304 | tf_op jit(solution)/shard_map/ppermute | solution.py:104
  173.1 1.9 copy-start.6
  175.0 0.9 copy-start.7
  175.9 18.9 %copy-start.8 = (f32[128]{0:T(128)S(1)}, f32[128]{0:T(128)}, u32[]{:S(2)}) copy-start(f32[128]{0:T(128)} %param.15) | copy-start | bytes 1540

commit v2 on v1

--- a/solution.py
+++ b/solution.py
@@ -6,6 +6,7 @@
 from jax.sharding import Mesh, PartitionSpec as P
 
 TILE = 128
+HALF = 64
 ROW_TILES = 8
 SLOTS = 128
 CHUNK = 16
@@ -31,9 +32,15 @@
         def _():
             fetch(c).start()
 
-    depth = pieces[0].shape[0]
-    for p, piece in enumerate(pieces):
-        feat[p * depth:(p + 1) * depth] = piece[...]
+    for side in range(2):
+        upper, lower = pieces[side], pieces[2 + side]
+        feat[48 * side:48 * side + 48, :HALF] = upper[...]
+
+        @pl.loop(0, 12)
+        def _(z):
+            for yh in range(4):
+                feat[48 * side + z * 4 + yh, HALF:] = lower[yh * 12 + z]
+
     acc[...] = jnp.zeros_like(acc)
     for c in range(chunks):
         @pl.when(c * CHUNK < live)
@@ -75,42 +82,42 @@
     )(count, rows, cols, tiles, *pieces)
 
 
-def dense_kernel(parts, w_first, b_first, w_second, out):
+def dense_kernel(parts, w_first, b_first, w_second, first, second):
     total = jnp.sum(parts[...].astype(jnp.float32), axis=0).astype(jnp.bfloat16)
     hidden = jnp.dot(total, w_first[...], preferred_element_type=jnp.float32)
     hidden = jnp.maximum(hidden + b_first[...], 0.0).astype(jnp.bfloat16)
     projected = jnp.dot(hidden, w_second[...], preferred_element_type=jnp.float32)
-    out[...] = jnp.broadcast_to(projected.astype(out.dtype)[None], out.shape)
+    projected = projected.astype(jnp.bfloat16)
+    first[...] = projected[:HALF]
+    second[...] = jnp.broadcast_to(projected[None, HALF:], second.shape)
 
 
 def dense(parts, w_first, b_first, w_second):
     return pl.pallas_call(
         dense_kernel,
-        out_shape=jax.ShapeDtypeStruct((4, TILE, TILE), jnp.bfloat16),
+        out_shape=[
+            jax.ShapeDtypeStruct((HALF, TILE), jnp.bfloat16),
+            jax.ShapeDtypeStruct((12, HALF, TILE), jnp.bfloat16),
+        ],
         in_specs=[pl.BlockSpec(memory_space=pltpu.VMEM)] * 4,
-        out_specs=pl.BlockSpec(memory_space=pltpu.VMEM),
+        out_specs=[pl.BlockSpec(memory_space=pltpu.VMEM)] * 2,
         name="dense",
     )(parts, w_first, b_first[None], w_second)
 
 
-def gather(copies):
-    column = lax.all_to_all(copies, "yh", 0, 0)
+def gather(first, second):
     swap = [(0, 1), (1, 0)]
-    own = []
-    other = []
-    for h in range(2):
-        half = lax.all_gather(column[2 * h:2 * h + 2], "z", axis=0, tiled=True)
-        own.append(half)
-        other.append(lax.ppermute(half, "core", swap))
-    return own + other
+    lines = lax.all_to_all(second, "z", 0, 0)
+    column = lax.all_gather(first, "yh", axis=0)
+    spread = lax.all_to_all(jnp.broadcast_to(lines[None], (4,) + lines.shape), "yh", 0, 0)
+    upper = lax.all_gather(column, "z", axis=0, tiled=True)
+    lower = spread.reshape(48, HALF, TILE)
+    return [upper, lax.ppermute(upper, "core", swap), lower, lax.ppermute(lower, "core", swap)]
 
 
 def position(cols):
     core = lax.axis_index("core")
-    z = cols // 8
-    yh = (cols // 2) % 4
-    piece = jnp.where(cols % 2 == core, 0, 2) + yh // 2
-    return piece * 24 + z * 2 + yh % 2
+    return jnp.where(cols % 2 == core, 0, 48) + cols // 2
 
 
 def local(features, tiles, tile_index, tile_count, w_first, b_first, w_second, b_second):
@@ -120,12 +127,12 @@
     rows = index // 96
     cols = position(index % 96)
 
-    def aggregate(copies):
-        partial = spmm(count, rows, cols, blocks, gather(copies))
+    def aggregate(first, second):
+        partial = spmm(count, rows, cols, blocks, gather(first, second))
         return lax.all_to_all(partial, COL, 0, 0)
 
-    first = aggregate(jnp.broadcast_to(features[None], (4, TILE, TILE)))
-    second = aggregate(dense(first, w_first, b_first, w_second))
+    first = aggregate(features[:HALF], jnp.broadcast_to(features[None, HALF:], (12, HALF, TILE)))
+    second = aggregate(*dense(first, w_first, b_first, w_second))
     return jnp.sum(second.astype(jnp.float32), axis=0) + b_second
 
 

time: 196 us -> 225 us (1.15)
  the two profiles are of different devices: /device:TPU:64 before, /device:TPU:1 now
where the time goes in v2:
time: 225 us; the launch traced here: 224 us
  blocking collectives  167 us (74%)
  starting transfers between devices  34.3 us (15%)
  Pallas kernels  13.1 us (6%)
  local copies, waits for them, and re-layouts  4.74 us (2%)
  waiting for transfers between devices  2.59 us (1%)
    all_gather x2, blocking collectives, gather(): column = lax.all_gather(first, 'yh', axis=0)  52.2 us
    all_to_all x2, blocking collectives, gather(): lines = lax.all_to_all(second, 'z', 0, 0)  46 us
    all_gather x2, blocking collectives, gather(): upper = lax.all_gather(column, 'z', axis=0, tiled=True)  45.9 us
    all_to_all x2, blocking collectives, aggregate(): return lax.all_to_all(partial, COL, 0, 0)  22.5 us
    ppermute x2, starting transfers between devices, gather(): lax.ppermute(upper, 'core', swap)  20 us
    pallas_call x2, Pallas kernels, spmm(): pl.pallas_call(spmm_kernel, out_shape=jax.ShapeDtypeStruct((ROW_TILES, TI...  11.2 us
    all_to_all x2, starting transfers between devices, gather(): lax.all_to_all(jnp.broadcast_to(lines[None], (4,) + lines.shape), 'yh', 0...  10.5 us
  transfers between devices with their start and end apart: 6, of which 2 were waited for; matrix products, arithmetic and copies ran while one was open for 1% of the time, Pallas kernels for 0%

profile of v2, /device:TPU:1, one launch (start us, length us, event | category | flops | bytes accessed | tf_op | source)
XLA Modules:
  0.0 224.2 jit_solution(11525795294562232627)
XLA Ops:
  0.0 0.7 fusion.2
  0.8 27.9 %all_to_all.30 = bf16[12,64,128]{2,1,0:T(8,128)(2,1)S(1)} all-to-all(bf16[12,64,128]{2,1,0:T(8,128)(2,1)S(1)} %broadcast_in_dim.15), channel_id=1, replica_groups=mesh['z'=12,'yh'=4,'core'=2,'x'=4,'yl'=2] {'z'}, dimensions={0} | all-to-all | bytes 393216 | tf_op jit(solution)/shard_map/all_to_all | solution.py:110
  28.7 1.1 broadcast_in_dim.16
  29.8 6.8 %all-to-all-start.1 = ((bf16[4,12,64,128]{3,2,1,0:T(8,128)(2,1)}), bf16[4,12,64,128]{3,2,1,0:T(8,128)(2,1)S(1)}, u32[]{:S(2)}, u32[]{:S(2)}) async-start(bf16[4,12,64,128]{3,2,1,0:T(8,128)(2,1)} %broadcast_in_dim.16), calls=%async_computation.1 | async-start | bytes 1572864 | tf_op jit(solution)/shard_map/all_to_all | solution.py:112
  36.6 26.2 %all-gather = bf16[256,128]{1,0:T(8,128)(2,1)S(1)} all-gather(bf16[64,128]{1,0:T(8,128)(2,1)S(1)} %get-tuple-element.10), channel_id=2, replica_groups=mesh['z'=12,'yh'=4,'core'=2,'x'=4,'yl'=2] {'yh'}, dimensions={0}, use_global_device_ids=true | all-gather | bytes 81920 | tf_op jit(solution)/shard_map/all_gather | solution.py:111
  62.9 23.0 %all_gather.20.rest_0_ = bf16[48,64,128]{2,1,0:T(8,128)(2,1)S(1)} all-gather(bf16[4,64,128]{2,1,0:T(8,128)(2,1)S(1)} %bitcast.26), channel_id=1, replica_groups=mesh['z'=12,'yh'=4,'core'=2,'x'=4,'yl'=2] {'z'}, dimensions={0}, use_global_device_ids=true | all-gather | bytes 851968 | tf_op jit(solution)/shard_map/all_gather | solution.py:113
  85.9 0.0 copy-start.2
  85.9 10.0 %collective-permute-start = (bf16[48,64,128]{2,1,0:T(8,128)(2,1)S(1)}, bf16[48,64,128]{2,1,0:T(8,128)(2,1)S(1)}, u32[]{:S(2)}, u32[]{:S(2)}) collective-permute-start(bf16[48,64,128]{2,1,0:T(8,128)(2,1)S(1)} %all_gather.20.rest_0_), channel_id=1, source_target_pairs={{0,8},{8,0},{1,9},{9,1},{2,10},{10,2},{3,11},{11,3},{4,12},{12,4},... | collective-permute-start | bytes 2359304 | tf_op jit(solution)/shard_map/ppermute | solution.py:115
  95.9 0.0 all-to-all-done.1
  95.9 0.0 copy-start
  95.9 1.9 collective-permute-start.1
  98.5 1.2 fusion.1
  99.7 0.0 collective-permute-done.rest_1_
  99.7 0.0 copy-start.4
  99.7 0.3 collective-permute-done.1.rest_3_
  100.1 0.0 copy-start.5
  100.1 0.0 copy-done.2
  100.1 0.0 copy-done
  100.1 0.5 copy-done.4
  100.6 0.3 copy-done.5
  101.0 5.6 %spmm.2 = bf16[8,128,128]{2,1,0:T(8,128)(2,1)} custom-call(s32[1]{0:T(128)} %bitcast.18.count, s32[128]{0:T(128)} %get-tuple-element.12.rows, s32[128]{0:T(128)} %get-tuple-element.11.cols, bf16[128,128,128]{2,1,0:T(8,128)(2,1)} %bitcast.20, bf16[48,64,128]{2,1,0:T(8,128)(2,1)} %copy-done.2, bf16[48,64,128]{2,1,0:T(8,128)(2,1)} %copy-done.4, ...), custom_call_target="tpu_custom_call" | custom-call | tf_op jit(solution)/shard_map/spmm/pallas_call | solution.py:70
  106.6 11.6 %all_to_all.31.parts = bf16[8,128,128]{2,1,0:T(8,128)(2,1)} all-to-all(bf16[8,128,128]{2,1,0:T(8,128)(2,1)} %spmm.2), channel_id=1, replica_groups=mesh['z'=12,'yh'=4,'core'=2,'x'=4,'yl'=2] {'x','yl'}, dimensions={0} | all-to-all | bytes 524288 | tf_op jit(solution)/shard_map/all_to_all | solution.py:132
  118.1 2.0 dense.1
  120.1 18.1 %all_to_all.32 = bf16[12,64,128]{2,1,0:T(8,128)(2,1)S(1)} all-to-all(bf16[12,64,128]{2,1,0:T(8,128)(2,1)} %get-tuple-element.8), channel_id=1, replica_groups=mesh['z'=12,'yh'=4,'core'=2,'x'=4,'yl'=2] {'z'}, dimensions={0} | all-to-all | bytes 393216 | tf_op jit(solution)/shard_map/all_to_all | solution.py:110
  138.2 1.1 broadcast_in_dim.32
  139.3 3.7 %all-to-all-start.4 = ((bf16[4,12,64,128]{3,2,1,0:T(8,128)(2,1)}), bf16[4,12,64,128]{3,2,1,0:T(8,128)(2,1)S(1)}, u32[]{:S(2)}, u32[]{:S(2)}) async-start(bf16[4,12,64,128]{3,2,1,0:T(8,128)(2,1)} %broadcast_in_dim.32), calls=%async_computation.4 | async-start | bytes 1572864 | tf_op jit(solution)/shard_map/all_to_all | solution.py:112
  143.0 26.0 %all-gather.1 = bf16[256,128]{1,0:T(8,128)(2,1)S(1)} all-gather(bf16[64,128]{1,0:T(8,128)(2,1)} %get-tuple-element.7), channel_id=3, replica_groups=mesh['z'=12,'yh'=4,'core'=2,'x'=4,'yl'=2] {'yh'}, dimensions={0}, use_global_device_ids=true | all-gather | bytes 81920 | tf_op jit(solution)/shard_map/all_gather | solution.py:111
  169.0 22.9 %all_gather.23.rest_0_ = bf16[48,64,128]{2,1,0:T(8,128)(2,1)S(1)} all-gather(bf16[4,64,128]{2,1,0:T(8,128)(2,1)S(1)} %bitcast.27), channel_id=1, replica_groups=mesh['z'=12,'yh'=4,'core'=2,'x'=4,'yl'=2] {'z'}, dimensions={0}, use_global_device_ids=true | all-gather | bytes 851968 | tf_op jit(solution)/shard_map/all_gather | solution.py:113
  191.9 0.0 copy-start.3
  191.9 10.0 %collective-permute-start.2 = (bf16[48,64,128]{2,1,0:T(8,128)(2,1)S(1)}, bf16[48,64,128]{2,1,0:T(8,128)(2,1)S(1)}, u32[]{:S(2)}, u32[]{:S(2)}) collective-permute-start(bf16[48,64,128]{2,1,0:T(8,128)(2,1)S(1)} %all_gather.23.rest_0_), channel_id=1, source_target_pairs={{0,8},{8,0},{1,9},{9,1},{2,10},{10,2},{3,11},{11,3},{4,12},{12,4},... | collective-permute-start | bytes 2359304 | tf_op jit(solution)/shard_map/ppermute | solution.py:115
  201.9 0.0 all-to-all-done.4
  201.9 0.0 copy-start.1
  201.9 1.9 collective-permute-start.3
  203.8 0.0 collective-permute-done.2.rest_1_
  203.8 0.0 copy-start.6
  203.8 2.2 collective-permute-done.3.rest_3_
  206.1 0.0 copy-start.7
  206.1 0.0 copy-done.3
  206.1 0.0 copy-done.1
  206.1 0.0 copy-done.6
  206.1 0.9 copy-done.7
  207.0 0.0 copy-start.8
  207.0 5.6 %spmm.3 = bf16[8,128,128]{2,1,0:T(8,128)(2,1)} custom-call(s32[1]{0:T(128)} %bitcast.19.count, s32[128]{0:T(128)} %get-tuple-element.12.rows, s32[128]{0:T(128)} %get-tuple-element.11.cols, bf16[128,128,128]{2,1,0:T(8,128)(2,1)} %bitcast.21, bf16[48,64,128]{2,1,0:T(8,128)(2,1)} %copy-done.3, bf16[48,64,128]{2,1,0:T(8,128)(2,1)} %copy-done.6, ...), custom_call_target="tpu_custom_call" | custom-call | tf_op jit(solution)/shard_map/spmm/pallas_call | solution.py:70
  212.6 10.9 %all_to_all.33 = bf16[8,128,128]{2,1,0:T(8,128)(2,1)S(1)} all-to-all(bf16[8,128,128]{2,1,0:T(8,128)(2,1)} %spmm.3), channel_id=1, replica_groups=mesh['z'=12,'yh'=4,'core'=2,'x'=4,'yl'=2] {'x','yl'}, dimensions={0} | all-to-all | bytes 524288 | tf_op jit(solution)/shard_map/all_to_all | solution.py:132
  223.5 0.0 copy-done.8
  223.5 0.6 broadcast_add_fusion
  (2 shorter events, 0.1 us)
Async XLA Ops:
  29.8 66.1 %all-to-all-start.1 = ((bf16[4,12,64,128]{3,2,1,0:T(8,128)(2,1)}), bf16[4,12,64,128]{3,2,1,0:T(8,128)(2,1)S(1)}, u32[]{:S(2)}, u32[]{:S(2)}) async-start(bf16[4,12,64,128]{3,2,1,0:T(8,128)(2,1)} %broadcast_in_dim.16), calls=%async_computation.1 | async-start | bytes 1572864 | tf_op jit(solution)/shard_map/all_to_all | solution.py:112
  85.9 14.2 %copy-start.2 = (bf16[48,64,128]{2,1,0:T(8,128)(2,1)}, bf16[48,64,128]{2,1,0:T(8,128)(2,1)S(1)}, u32[]{:S(2)}) copy-start(bf16[48,64,128]{2,1,0:T(8,128)(2,1)S(1)} %all_gather.20.rest_0_) | copy-start | bytes 2359300
  85.9 13.9 %collective-permute-start = (bf16[48,64,128]{2,1,0:T(8,128)(2,1)S(1)}, bf16[48,64,128]{2,1,0:T(8,128)(2,1)S(1)}, u32[]{:S(2)}, u32[]{:S(2)}) collective-permute-start(bf16[48,64,128]{2,1,0:T(8,128)(2,1)S(1)} %all_gather.20.rest_0_), channel_id=1, source_target_pairs={{0,8},{8,0},{1,9},{9,1},{2,10},{10,2},{3,11},{11,3},{4,12},{12,4},... | collective-permute-start | bytes 2359304 | tf_op jit(solution)/shard_map/ppermute | solution.py:115
  95.9 4.2 %copy-start = (bf16[4,12,64,128]{3,2,1,0:T(8,128)(2,1)}, bf16[4,12,64,128]{3,2,1,0:T(8,128)(2,1)S(1)}, u32[]{:S(2)}) copy-start(bf16[4,12,64,128]{3,2,1,0:T(8,128)(2,1)S(1)} %all-to-all-done.1) | copy-start | bytes 2359300
  95.9 4.2 %collective-permute-start.1 = (bf16[48,64,128]{2,1,0:T(8,128)(2,1)S(1)}, bf16[48,64,128]{2,1,0:T(8,128)(2,1)S(1)}, u32[]{:S(2)}, u32[]{:S(2)}) collective-permute-start(bf16[48,64,128]{2,1,0:T(8,128)(2,1)S(1)} %bitcast.22), channel_id=1, source_target_pairs={{0,8},{8,0},{1,9},{9,1},{2,10},{10,2},{3,11},{11,3},{4,12},{12,4},... | collective-permute-start | bytes 2359304 | tf_op jit(solution)/shard_map/ppermute | solution.py:115
  99.7 0.9 copy-start.4
  100.1 0.9 copy-start.5
  139.3 62.6 %all-to-all-start.4 = ((bf16[4,12,64,128]{3,2,1,0:T(8,128)(2,1)}), bf16[4,12,64,128]{3,2,1,0:T(8,128)(2,1)S(1)}, u32[]{:S(2)}, u32[]{:S(2)}) async-start(bf16[4,12,64,128]{3,2,1,0:T(8,128)(2,1)} %broadcast_in_dim.32), calls=%async_computation.4 | async-start | bytes 1572864 | tf_op jit(solution)/shard_map/all_to_all | solution.py:112
  191.9 14.2 %copy-start.3 = (bf16[48,64,128]{2,1,0:T(8,128)(2,1)}, bf16[48,64,128]{2,1,0:T(8,128)(2,1)S(1)}, u32[]{:S(2)}) copy-start(bf16[48,64,128]{2,1,0:T(8,128)(2,1)S(1)} %all_gather.23.rest_0_) | copy-start | bytes 2359300
  191.9 12.0 %collective-permute-start.2 = (bf16[48,64,128]{2,1,0:T(8,128)(2,1)S(1)}, bf16[48,64,128]{2,1,0:T(8,128)(2,1)S(1)}, u32[]{:S(2)}, u32[]{:S(2)}) collective-permute-start(bf16[48,64,128]{2,1,0:T(8,128)(2,1)S(1)} %all_gather.23.rest_0_), channel_id=1, source_target_pairs={{0,8},{8,0},{1,9},{9,1},{2,10},{10,2},{3,11},{11,3},{4,12},{12,4},... | collective-permute-start | bytes 2359304 | tf_op jit(solution)/shard_map/ppermute | solution.py:115
  201.9 4.2 %copy-start.1 = (bf16[4,12,64,128]{3,2,1,0:T(8,128)(2,1)}, bf16[4,12,64,128]{3,2,1,0:T(8,128)(2,1)S(1)}, u32[]{:S(2)}) copy-start(bf16[4,12,64,128]{3,2,1,0:T(8,128)(2,1)S(1)} %all-to-all-done.4) | copy-start | bytes 2359300
  201.9 4.2 %collective-permute-start.3 = (bf16[48,64,128]{2,1,0:T(8,128)(2,1)S(1)}, bf16[48,64,128]{2,1,0:T(8,128)(2,1)S(1)}, u32[]{:S(2)}, u32[]{:S(2)}) collective-permute-start(bf16[48,64,128]{2,1,0:T(8,128)(2,1)S(1)} %bitcast.24), channel_id=1, source_target_pairs={{0,8},{8,0},{1,9},{9,1},{2,10},{10,2},{3,11},{11,3},{4,12},{12,4},... | collective-permute-start | bytes 2359304 | tf_op jit(solution)/shard_map/ppermute | solution.py:115
  203.8 2.3 %copy-start.6 = (bf16[48,64,128]{2,1,0:T(8,128)(2,1)}, bf16[48,64,128]{2,1,0:T(8,128)(2,1)S(1)}, u32[]{:S(2)}) copy-start(bf16[48,64,128]{2,1,0:T(8,128)(2,1)S(1)} %collective-permute-done.2.rest_1_) | copy-start | bytes 2359300
  206.1 0.9 copy-start.7
  207.0 16.6 %copy-start.8 = (f32[128]{0:T(128)S(1)}, f32[128]{0:T(128)}, u32[]{:S(2)}) copy-start(f32[128]{0:T(128)} %param.15) | copy-start | bytes 1540
